TPU v7x, 128 devices: a whole 4x4x4 slice. The times are simulated.
128 devices in a mesh: row: 16 (over y, x), col: 8 (over z, core).
Axes of the slice: x: 4, y: 4, z: 4, core: 2. Of those that a mesh axis runs over, the one named last changes fastest.
Arguments:
- layer_input: bfloat16 [768, 8192], P('col', 'row'), may hold values from -6 to 6
- out_grad: bfloat16 [768, 8192], P('col', 'row'), may hold values from -6 to 6
- gate_weight: bfloat16 [8192, 28672], P('row', 'col'), may hold values from -0.0625 to 0.0625
- up_weight: bfloat16 [8192, 28672], P('row', 'col'), may hold values from -0.0625 to 0.0625
- down_weight: bfloat16 [28672, 8192], P('col', 'row'), may hold values from -0.03125 to 0.03125
Outputs:
- input_grad: bfloat16 [768, 8192], P('col', 'row')
- gate_grad: bfloat16 [8192, 28672], P('row', 'col')
- up_grad: bfloat16 [8192, 28672], P('row', 'col')
- down_grad: bfloat16 [28672, 8192], P('col', 'row')
All inputs are finite; a program needn't handle non-finite values.
Results may differ from a plain program's by a relative error of at most 0.033.
Values may be sent and summed in bfloat16 or wider, within the bound.
A program may use at most 192 MiB of HBM per device.

v0:
```python
import jax
import jax.numpy as jnp
from jax import lax
from jax.sharding import PartitionSpec as P


def swiglu_back(summed, width):
    gate = summed[:, :width]
    up = summed[:, width : 2 * width]
    hidden_grad = summed[:, 2 * width :]
    sigma = jax.nn.sigmoid(gate)
    swish = gate * sigma
    hidden = (swish * up).astype(jnp.bfloat16)
    up_delta = (hidden_grad * swish).astype(jnp.bfloat16)
    gate_delta = (hidden_grad * up * sigma * (1.0 + gate * (1.0 - sigma))).astype(jnp.bfloat16)
    return (hidden, gate_delta, up_delta)


def local(layer_input, out_grad, gate_weight, up_weight, down_weight):
    input_rows, cot_rows = (
        lax.all_gather(layer_input, "col", axis=0, tiled=True),
        lax.all_gather(out_grad, "col", axis=0, tiled=True),
    )
    tokens = input_rows.shape[0]
    width = gate_weight.shape[1]
    both_weights = jnp.concatenate([gate_weight, up_weight], axis=1)
    contract_last = (((1,), (1,)), ((), ()))
    contract_first = (((0,), (0,)), ((), ()))
    left = input_rows
    right = cot_rows
    gate_up = jnp.dot(left, both_weights, preferred_element_type=jnp.float32)
    hidden_grad = lax.dot_general(
        right, down_weight, contract_last, preferred_element_type=jnp.float32
    )
    summed = lax.psum_scatter(
        jnp.concatenate([gate_up, hidden_grad], axis=1).astype(jnp.bfloat16),
        "row",
        scatter_dimension=0,
        tiled=True,
    ).astype(jnp.float32)
    hidden, gate_delta, up_delta = swiglu_back(summed, width)
    accumulate_hidden = lax.all_gather(hidden, "row", axis=0, tiled=True)
    accumulate_gate_delta = lax.all_gather(gate_delta, "row", axis=0, tiled=True)
    accumulate_up_delta = lax.all_gather(up_delta, "row", axis=0, tiled=True)
    left = input_rows
    right = cot_rows
    down_sum = lax.dot_general(
        accumulate_hidden, right, contract_first, preferred_element_type=jnp.float32
    )
    gate_sum = lax.dot_general(
        left, accumulate_gate_delta, contract_first, preferred_element_type=jnp.float32
    )
    up_sum = lax.dot_general(
        left, accumulate_up_delta, contract_first, preferred_element_type=jnp.float32
    )
    term = lax.dot_general(
        accumulate_gate_delta, gate_weight, contract_last, preferred_element_type=jnp.float32
    )
    term = term + lax.dot_general(
        accumulate_up_delta, up_weight, contract_last, preferred_element_type=jnp.float32
    )
    factor = 1.0 / tokens**0.5
    down_grad = (down_sum * factor).astype(jnp.bfloat16)
    gate_grad = (gate_sum * factor).astype(jnp.bfloat16)
    up_grad = (up_sum * factor).astype(jnp.bfloat16)
    input_grad = lax.psum_scatter(term.astype(jnp.bfloat16), "col", scatter_dimension=0, tiled=True)
    return (input_grad, gate_grad, up_grad, down_grad)


def solution(mesh):
    placed = (P("col", "row"), P("col", "row"), P("row", "col"), P("row", "col"), P("col", "row"))
    return jax.shard_map(
        local,
        mesh=mesh,
        in_specs=placed,
        out_specs=(P("col", "row"), P("row", "col"), P("row", "col"), P("col", "row")),
        check_vma=False,
    )
```

profile of v0, /device:TPU:1, one launch (start us, length us, event | category | flops | bytes accessed | tf_op | source)
XLA Modules:
  0.0 427.0 jit_solution(3540597175312089114)
XLA Ops:
  7.2 0.0 reduce-scatter.7.cloned.1.call-start
  7.2 16.1 %all_gather.15 = bf16[768,512]{1,0:T(8,128)(2,1)S(1)} all-gather(bf16[96,512]{1,0:T(8,128)(2,1)} %param.5), channel_id=1, replica_groups=mesh['row'=16,'col'=8] {'col'}, dimensions={0}, use_global_device_ids=true | all-gather | bytes 884736 | tf_op jit(solution)/shard_map/all_gather | solution.py:21
  23.4 13.6 %all_gather.16 = bf16[768,512]{1,0:T(8,128)(2,1)S(1)} all-gather(bf16[96,512]{1,0:T(8,128)(2,1)} %param.6), channel_id=1, replica_groups=mesh['row'=16,'col'=8] {'col'}, dimensions={0}, use_global_device_ids=true | all-gather | bytes 884736 | tf_op jit(solution)/shard_map/all_gather | solution.py:22
  37.0 7.5 %convolution_convert_fusion.1 = bf16[768,3584]{0,1:T(8,128)(2,1)} fusion(bf16[768,512]{1,0:T(8,128)(2,1)S(1)} %all_gather.16, bf16[3584,512]{1,0:T(8,128)(2,1)} %param.9), kind=kOutput, calls=%fused_computation.9 | convolution fusion | flops 2821324800 | bytes 9961472 | tf_op jit(solution)/shard_map/dot_general | solution.py:32
  44.4 13.8 %fusion = bf16[768,7168]{0,1:T(8,128)(2,1)} fusion(bf16[768,512]{1,0:T(8,128)(2,1)S(1)} %all_gather.15, bf16[512,3584]{1,0:T(8,128)(2,1)} %param.8, bf16[512,3584]{1,0:T(8,128)(2,1)} %param.7), kind=kOutput, calls=%fused_computation.2 | convolution fusion | flops 5657329664 | bytes 19136512 | tf_op jit(solution)/shard_map/dot_general | solution.py:31
  58.2 18.5 %pad_maximum_fusion = bf16[768,10752]{0,1:T(8,128)(2,1)} fusion(bf16[768,3584]{0,1:T(8,128)(2,1)} %convolution_convert_fusion.1, bf16[768,7168]{0,1:T(8,128)(2,1)} %fusion), kind=kLoop, calls=%fused_computation | loop fusion | flops 33030144 | bytes 33030144 | tf_op jit(solution)/shard_map/concatenate | solution.py:36
  76.7 22.3 %copy.23 = bf16[768,10752]{1,0:T(8,128)(2,1)} copy(bf16[768,10752]{0,1:T(8,128)(2,1)} %pad_maximum_fusion) | data formatting | bytes 33030144
  99.1 0.0 reduce-scatter.7.cloned.1.call-update
  99.1 0.0 all-gather.4.cloned.1.call-start
  99.1 109.8 %reduce-scatter.7.cloned.1.call-done = bf16[48,10752]{1,0:T(8,128)(2,1)} async-done(((bf16[768,10752]{1,0:T(8,128)(2,1)}), bf16[48,10752]{1,0:T(8,128)(2,1)}) %reduce-scatter.7.cloned.1.call-update) | async-done | bytes 1032208 | tf_op jit(solution)/shard_map/reduce_scatter | solution.py:35
  209.0 1.4 convert_element_type.31
  210.3 1.3 multiply_convert_fusion.3
  211.6 0.0 all-gather.4.cloned.1.call-update
  211.6 0.0 all-gather.6.cloned.1.call-start
  211.7 0.7 all-gather.6.cloned.1.call-update
  212.4 0.0 all-gather.8.cloned.1.call-start
  212.4 0.5 all-gather.8.cloned.1.call-update
  213.0 0.2 reduce-scatter.5.cloned.1.call-start
  213.2 56.2 %all-gather.4.cloned.1.call-done = bf16[768,3584]{1,0:T(8,128)(2,1)} async-done(((bf16[48,3584]{1,0:T(8,128)(2,1)}), bf16[768,3584]{1,0:T(8,128)(2,1)}) %all-gather.4.cloned.1.call-update) | async-done | bytes 5505040 | tf_op jit(solution)/shard_map/all_gather | solution.py:43
  269.4 6.1 %fusion.8 = f32[768,512]{1,0:T(8,128)S(1)} fusion(bf16[768,3584]{1,0:T(8,128)(2,1)} %all-gather.4.cloned.1.call-done, bf16[512,3584]{1,0:T(8,128)(2,1)} %param.7), kind=kOutput, calls=%fused_computation.19 | convolution fusion | flops 2818572288 | bytes 10747904 | tf_op jit(solution)/shard_map/dot_general | solution.py:56
  275.5 54.1 %all-gather.6.cloned.1.call-done = bf16[768,3584]{1,0:T(8,128)(2,1)} async-done(((bf16[48,3584]{1,0:T(8,128)(2,1)}), bf16[768,3584]{1,0:T(8,128)(2,1)}) %all-gather.6.cloned.1.call-update) | async-done | bytes 5505040 | tf_op jit(solution)/shard_map/all_gather | solution.py:44
  329.6 7.6 %add_convert_fusion = bf16[768,512]{1,0:T(8,128)(2,1)} fusion(f32[768,512]{1,0:T(8,128)S(1)} %fusion.8, bf16[768,3584]{1,0:T(8,128)(2,1)} %all-gather.6.cloned.1.call-done, bf16[512,3584]{1,0:T(8,128)(2,1)} %param.8), kind=kOutput, calls=%fused_computation.12 | convolution fusion | flops 2819358720 | bytes 11534336 | tf_op jit(solution)/shard_map/dot_general | solution.py:59
  337.2 0.0 reduce-scatter.5.cloned.1.call-update
  337.2 7.1 %fusion.5 = bf16[512,3584]{0,1:T(8,128)(2,1)} fusion(bf16[768,3584]{1,0:T(8,128)(2,1)} %all-gather.6.cloned.1.call-done, bf16[768,512]{1,0:T(8,128)(2,1)S(1)} %all_gather.15), kind=kOutput, calls=%fused_computation.11 | convolution fusion | flops 2822242304 | bytes 9961472 | tf_op jit(solution)/shard_map/dot_general | solution.py:53
  344.3 5.9 %copy.21 = bf16[512,3584]{1,0:T(8,128)(2,1)} copy(bf16[512,3584]{0,1:T(8,128)(2,1)} %fusion.5) | data formatting | bytes 7340032
  350.3 7.2 %fusion.4 = bf16[512,3584]{0,1:T(8,128)(2,1)} fusion(bf16[768,3584]{1,0:T(8,128)(2,1)} %all-gather.4.cloned.1.call-done, bf16[768,512]{1,0:T(8,128)(2,1)S(1)} %all_gather.15), kind=kOutput, calls=%fused_computation.10 | convolution fusion | flops 2822242304 | bytes 9961472 | tf_op jit(solution)/shard_map/dot_general | solution.py:50
  357.4 5.9 %copy.20 = bf16[512,3584]{1,0:T(8,128)(2,1)} copy(bf16[512,3584]{0,1:T(8,128)(2,1)} %fusion.4) | data formatting | bytes 7340032
  363.3 25.8 %all-gather.8.cloned.1.call-done = bf16[768,3584]{1,0:T(8,128)(2,1)} async-done(((bf16[48,3584]{1,0:T(8,128)(2,1)}), bf16[768,3584]{1,0:T(8,128)(2,1)}) %all-gather.8.cloned.1.call-update) | async-done | bytes 5505040 | tf_op jit(solution)/shard_map/all_gather | solution.py:42
  389.1 7.1 %multiply_convert_fusion = bf16[3584,512]{1,0:T(8,128)(2,1)} fusion(bf16[768,3584]{1,0:T(8,128)(2,1)} %all-gather.8.cloned.1.call-done, bf16[768,512]{1,0:T(8,128)(2,1)S(1)} %all_gather.16), kind=kOutput, calls=%fused_computation.6 | convolution fusion | flops 2822242304 | bytes 9961472 | tf_op jit(solution)/shard_map/dot_general | solution.py:47
  396.2 24.3 %reduce-scatter.5.cloned.1.call-done = bf16[96,512]{1,0:T(8,128)(2,1)} async-done(((bf16[768,512]{1,0:T(8,128)(2,1)}), bf16[96,512]{1,0:T(8,128)(2,1)}) %reduce-scatter.5.cloned.1.call-update) | async-done | bytes 98320 | tf_op jit(solution)/shard_map/reduce_scatter | solution.py:66
Async XLA Ops:
  7.2 201.8 %reduce-scatter.7.cloned.1.call-start = ((), (), s32[]{:S(2)}) async-start(), calls=%async_computation.6 | async-start | bytes 17547264 | tf_op jit(solution)/shard_map/reduce_scatter | solution.py:35
  99.1 170.3 %all-gather.4.cloned.1.call-start = ((), (), s32[]{:S(2)}) async-start(), calls=%async_computation.2 | async-start | bytes 5849088 | tf_op jit(solution)/shard_map/all_gather | solution.py:43
  211.6 117.9 %all-gather.6.cloned.1.call-start = ((), (), s32[]{:S(2)}) async-start(), calls=%async_computation.3 | async-start | bytes 5849088 | tf_op jit(solution)/shard_map/all_gather | solution.py:44
  212.4 176.7 %all-gather.8.cloned.1.call-start = ((), (), s32[]{:S(2)}) async-start(), calls=%async_computation.5 | async-start | bytes 5849088 | tf_op jit(solution)/shard_map/all_gather | solution.py:42
  213.0 207.5 %reduce-scatter.5.cloned.1.call-start = ((), (), s32[]{:S(2)}) async-start(), calls=%async_computation.4 | async-start | bytes 884736 | tf_op jit(solution)/shard_map/reduce_scatter | solution.py:66
Sparse Core Ops, SparseCore 0:
  99.2 109.7 reduce-scatter.6
  211.9 57.4 all-gather.3
  272.3 57.2 all-gather.5
  331.8 57.2 all-gather.7
  392.0 28.3 reduce-scatter.4
where the time goes:
time: 430 us; the launch traced here: 427 us
  waiting for transfers between devices  271 us (63%)
  matrix products  56.3 us (13%)
  local copies, waits for them, and re-layouts  34.2 us (8%)
  blocking collectives  29.8 us (7%)
  other arithmetic  21.2 us (5%)
  between operations  13.8 us (3%)
    reduce_scatter x1, waiting for transfers between devices, local(): lax.psum_scatter(jnp.concatenate([gate_up, hidden_grad], axis=1).astype(j...  110 us
    all_gather x1, waiting for transfers between devices, local(): lax.all_gather(gate_delta, 'row', axis=0, tiled=True)  56.2 us
    all_gather x1, waiting for transfers between devices, local(): accumulate_up_delta = lax.all_gather(up_delta, 'row', axis=0, tiled=True)  54.1 us
    unnamed x3, local copies, waits for them, and re-layouts  34.2 us
    all_gather x1, waiting for transfers between devices, local(): accumulate_hidden = lax.all_gather(hidden, 'row', axis=0, tiled=True)  25.8 us
    reduce_scatter x1, waiting for transfers between devices, local(): lax.psum_scatter(term.astype(jnp.bfloat16), 'col', scatter_dimension=0, t...  24.3 us
    concatenate x1, other arithmetic, local(): jnp.concatenate([gate_up, hidden_grad], axis=1).astype(jnp.bfloat16)  18.5 us
    all_gather x1, blocking collectives, local(): lax.all_gather(layer_input, 'col', axis=0, tiled=True)  16.1 us
  transfers between devices with their start and end apart: 5, of which 5 were waited for; matrix products, arithmetic and copies ran while one was open for 11% of the time, Pallas kernels for 0%

commit v1 on v0

v1 whole, which is shorter than its diff:
```python
import jax
import jax.numpy as jnp
from jax import lax
from jax.experimental import pallas as pl
from jax.experimental.pallas import tpu as pltpu
from jax.sharding import PartitionSpec as P

MESH = pl.DeviceIdType.MESH
BF = jnp.bfloat16
F32 = jnp.float32
NT = (((1,), (1,)), ((), ()))
TN = (((0,), (0,)), ((), ()))
GROUPS = 4
ROWS = 192
HALF = 96
SIDE = 4
BLOCK = 512
SLOTS = 12
LAG = 2


def stream_kernel(
    x_hbm, dy_hbm, wg_hbm, wu_hbm, wd_hbm,
    out_ref, g_hbm, xo_hbm,
    wg, wu, wd, xb, part, r1, r2, r3, r4, full, acc, stage, landed,
    w_sem, x_sem, xs_sem, xr_sem, ssem, rsem, is_sem, ir_sem, g_sem, xo_sem,
):
    blocks = wg.shape[1] // BLOCK
    units = GROUPS * blocks
    row = lax.axis_index("row")
    col = lax.axis_index("col")
    y, x = row // SIDE, lax.rem(row, SIDE)
    z, core = col // 2, lax.rem(col, 2)

    def add(a, n):
        return lax.rem(a + n, 4)

    def weight_copies(j):
        cols = pl.ds(pl.multiple_of(j * BLOCK, BLOCK), BLOCK)
        return (
            pltpu.make_async_copy(wg_hbm.at[:, cols], wg.at[:, cols], w_sem.at[0, j]),
            pltpu.make_async_copy(wu_hbm.at[:, cols], wu.at[:, cols], w_sem.at[1, j]),
            pltpu.make_async_copy(wd_hbm.at[cols, :], wd.at[cols, :], w_sem.at[2, j]),
        )

    own = (
        pltpu.make_async_copy(x_hbm, xb.at[col, 0], x_sem.at[0]),
        pltpu.make_async_copy(dy_hbm, xb.at[col, 1], x_sem.at[1]),
    )
    for c in own:
        c.start()

    @pl.loop(0, blocks)
    def _(j):
        for c in weight_copies(j):
            c.start()

    partners = [(z, 1 - core)] + [(add(z, 4 - d), k) for d in (1, 2, 3) for k in (0, 1)]
    around = [(y, add(x, 1)), (y, add(x, 3)), (add(y, 1), x), (add(y, 3), x)]
    barrier = pltpu.get_barrier_semaphore()
    for pz, pk in partners:
        pl.semaphore_signal(barrier, inc=1, device_id=(row, pz * 2 + pk), device_id_type=MESH)
    for py, px in around:
        pl.semaphore_signal(barrier, inc=1, device_id=(py * SIDE + px, col), device_id_type=MESH)
    pl.semaphore_wait(barrier, len(partners) + len(around))

    for c in own:
        c.wait()

    def shard_copy(n, source):
        pz, pk = partners[n]
        return pltpu.make_async_remote_copy(
            src_ref=xb.at[col], dst_ref=xb.at[source], send_sem=xs_sem.at[n], recv_sem=xr_sem.at[source],
            device_id=(row, pz * 2 + pk), device_id_type=MESH,
        )

    for n in range(len(partners)):
        shard_copy(n, col).start()
    shard_copy(0, z * 2 + 1 - core).wait_recv()

    def token_copy(s):
        group = add(z, s)
        return pltpu.make_async_copy(xb.at[pl.ds(group * 2, 2)], xo_hbm.at[s], xo_sem.at[s])

    def grad_copy(u):
        return pltpu.make_async_copy(full.at[u], g_hbm.at[u], g_sem.at[u])

    def term_copy(s, k):
        return pltpu.make_async_remote_copy(
            src_ref=stage.at[s, k], dst_ref=landed.at[col], send_sem=is_sem.at[s, k], recv_sem=ir_sem.at[col],
            device_id=(row, add(z, s) * 2 + k), device_id_type=MESH,
        )

    @pl.loop(0, units + 8 * LAG)
    def _(t):
        odd = lax.rem(t, 2)
        i1 = jnp.where(odd == 0, x, y)
        i2 = jnp.where(odd == 0, y, x)

        def device(d1, d2):
            a, b = add(i1, d1), add(i2, d2)
            ny, nx = jnp.where(odd == 0, b, a), jnp.where(odd == 0, a, b)
            return (ny * SIDE + nx, col)

        up1, down1, up2, down2 = device(1, 0), device(3, 0), device(0, 1), device(0, 3)
        n1, p1, f1 = add(i1, 1), add(i1, 3), add(i1, 2)
        n2, p2, f2 = add(i2, 1), add(i2, 3), add(i2, 2)

        def send(u, slot, m):
            src, dst, target = {
                0: (lambda: part.at[slot, f1, pl.ds(0, 2)], lambda: r1.at[slot, 0], up1),
                1: (lambda: part.at[slot, f1, pl.ds(2, 2)], lambda: r1.at[slot, 1], down1),
                2: (lambda: part.at[slot, n1], lambda: r2.at[slot, 0], up1),
                3: (lambda: part.at[slot, p1], lambda: r2.at[slot, 1], down1),
                4: (lambda: part.at[slot, i1, f2, pl.ds(0, 5)], lambda: r3.at[slot, pl.ds(0, 5)], up2),
                5: (lambda: part.at[slot, i1, f2, pl.ds(5, 4)], lambda: r3.at[slot, pl.ds(5, 4)], down2),
                6: (lambda: part.at[slot, i1, n2], lambda: r4.at[slot, 0], up2),
                7: (lambda: part.at[slot, i1, p2], lambda: r4.at[slot, 1], down2),
                8: (lambda: full.at[u, i1, i2], lambda: full.at[u, i1, i2], up2),
                9: (lambda: full.at[u, i1, i2], lambda: full.at[u, i1, i2], down2),
                10: (lambda: full.at[u, i1, p2, pl.ds(0, 5)], lambda: full.at[u, i1, p2, pl.ds(0, 5)], up2),
                11: (lambda: full.at[u, i1, n2, pl.ds(5, 4)], lambda: full.at[u, i1, n2, pl.ds(5, 4)], down2),
                12: (lambda: full.at[u, i1], lambda: full.at[u, i1], up1),
                13: (lambda: full.at[u, i1], lambda: full.at[u, i1], down1),
                14: (lambda: full.at[u, p1, pl.ds(0, 2)], lambda: full.at[u, p1, pl.ds(0, 2)], up1),
                15: (lambda: full.at[u, n1, pl.ds(2, 2)], lambda: full.at[u, n1, pl.ds(2, 2)], down1),
            }[m]
            return pltpu.make_async_remote_copy(
                src_ref=src(), dst_ref=dst(), send_sem=ssem.at[slot, m], recv_sem=rsem.at[slot, m],
                device_id=target, device_id_type=MESH,
            )

        def at_stage(k):
            u = t - k * LAG

            def run(body):
                @pl.when(jnp.logical_and(u >= 0, u < units))
                def _():
                    body(u, lax.rem(u, SLOTS))
            return run

        @at_stage(7)
        def _(u, slot):
            send(u, slot, 12).wait()
            send(u, slot, 14).start()
            send(u, slot, 13).wait()
            send(u, slot, 15).start()

        @at_stage(6)
        def _(u, slot):
            send(u, slot, 10).wait()
            send(u, slot, 11).wait()
            send(u, slot, 12).start()
            send(u, slot, 13).start()

        @at_stage(5)
        def _(u, slot):
            send(u, slot, 8).wait()
            send(u, slot, 10).start()
            send(u, slot, 9).wait()
            send(u, slot, 11).start()

        @at_stage(4)
        def _(u, slot):
            send(u, slot, 6).wait()
            send(u, slot, 7).wait()
            total = (
                part[slot, i1, i2].astype(F32) + r4[slot, 0].astype(F32) + r4[slot, 1].astype(F32)
            )
            gate, up, hidden_grad = total[0:3], total[3:6], total[6:9]
            sigma = 1.0 / (1.0 + jnp.exp(-gate))
            swish = gate * sigma
            full[u, i1, i2, 0:3] = (swish * up).astype(BF)
            full[u, i1, i2, 3:6] = (hidden_grad * up * sigma * (1.0 + gate * (1.0 - sigma))).astype(BF)
            full[u, i1, i2, 6:9] = (hidden_grad * swish).astype(BF)
            send(u, slot, 8).start()
            send(u, slot, 9).start()

        @at_stage(3)
        def _(u, slot):
            send(u, slot, 4).wait()
            part[slot, i1, n2, 0:5] = (part[slot, i1, n2, 0:5].astype(F32) + r3[slot, 0:5].astype(F32)).astype(BF)
            send(u, slot, 6).start()
            send(u, slot, 5).wait()
            part[slot, i1, p2, 5:9] = (part[slot, i1, p2, 5:9].astype(F32) + r3[slot, 5:9].astype(F32)).astype(BF)
            send(u, slot, 7).start()

        @at_stage(2)
        def _(u, slot):
            send(u, slot, 2).wait()
            send(u, slot, 3).wait()
            part[slot, i1] = (
                part[slot, i1].astype(F32) + r2[slot, 0].astype(F32) + r2[slot, 1].astype(F32)
            ).astype(BF)
            send(u, slot, 4).start()
            send(u, slot, 5).start()

        @at_stage(1)
        def _(u, slot):
            send(u, slot, 0).wait()
            part[slot, n1, 0:2] = (part[slot, n1, 0:2].astype(F32) + r1[slot, 0].astype(F32)).astype(BF)
            send(u, slot, 2).start()
            send(u, slot, 1).wait()
            part[slot, p1, 2:4] = (part[slot, p1, 2:4].astype(F32) + r1[slot, 1].astype(F32)).astype(BF)
            send(u, slot, 3).start()

        @at_stage(0)
        def _(u, slot):
            s, j = u // blocks, lax.rem(u, blocks)
            group = add(z, s)

            @pl.when(s == 0)
            def _():
                for c in weight_copies(j):
                    c.wait()

            @pl.when(jnp.logical_and(s > 0, j == 0))
            def _():
                for k in (0, 1):
                    shard_copy(1, group * 2 + k).wait_recv()

            @pl.when(j == 0)
            def _():
                token_copy(s).start()

            cols = pl.ds(pl.multiple_of(j * BLOCK, BLOCK), BLOCK)
            for arr in range(3):
                left = xb[pl.ds(group * 2, 2), arr // 2].reshape(ROWS, BLOCK)
                if arr == 0:
                    term = jnp.dot(left, wg[:, cols], preferred_element_type=F32)
                elif arr == 1:
                    term = jnp.dot(left, wu[:, cols], preferred_element_type=F32)
                else:
                    term = lax.dot_general(left, wd[cols, :], NT, preferred_element_type=F32)
                term = term.astype(BF)
                for a in range(4):
                    part[slot, a, :, 3 * arr : 3 * arr + 3] = term[:, 128 * a : 128 * a + 128].reshape(4, 3, 16, 128)
            send(u, slot, 0).start()
            send(u, slot, 1).start()

        @at_stage(8)
        def _(u, slot):
            s, j = u // blocks, lax.rem(u, blocks)
            send(u, slot, 14).wait()
            send(u, slot, 15).wait()
            grad_copy(u).start()

            @pl.when(j == 0)
            def _():
                acc[...] = jnp.zeros_like(acc)

            cols = pl.ds(pl.multiple_of(j * BLOCK, BLOCK), BLOCK)
            total = acc[...]
            for arr, weight in ((1, wg), (2, wu)):
                left = jnp.concatenate(
                    [full[u, a, :, 3 * arr : 3 * arr + 3].reshape(ROWS, 128) for a in range(4)], axis=1
                )
                total = total + lax.dot_general(left, weight[:, cols], NT, preferred_element_type=F32)
            acc[...] = total

            @pl.when(j == blocks - 1)
            def _():
                for k in (0, 1):
                    mine = jnp.logical_and(s == 0, core == k)

                    @pl.when(mine)
                    def _():
                        landed[col] = acc[HALF * k : HALF * (k + 1)].astype(BF)

                    @pl.when(jnp.logical_not(mine))
                    def _():
                        stage[s, k] = acc[HALF * k : HALF * (k + 1)].astype(BF)
                        term_copy(s, k).start()

    total = landed[col].astype(F32)
    for pz, pk in partners:
        source = pz * 2 + pk
        pltpu.make_async_remote_copy(
            src_ref=stage.at[0, 0], dst_ref=landed.at[source], send_sem=is_sem.at[0, 0], recv_sem=ir_sem.at[source],
            device_id=(row, source), device_id_type=MESH,
        ).wait_recv()
        total = total + landed[source].astype(F32)
    out_ref[...] = total.astype(BF)

    for n in range(len(partners)):
        shard_copy(n, col).wait_send()
    for s in range(GROUPS):
        token_copy(s).wait()
        for k in (0, 1):
            @pl.when(jnp.logical_not(jnp.logical_and(s == 0, core == k)))
            def _():
                term_copy(s, k).wait_send()

    @pl.loop(0, units)
    def _(u):
        grad_copy(u).wait()


def weight_kernel(factor, g_ref, x_ref, gate_ref, up_ref, down_ref, xt, dy):
    tokens = GROUPS * ROWS

    @pl.when(pl.program_id(0) == 0)
    def _():
        xt[...] = x_ref[:, :, 0].reshape(tokens, BLOCK).T
        dy[...] = x_ref[:, :, 1].reshape(tokens, BLOCK)

    def gathered(arr):
        return jnp.concatenate(
            [g_ref[:, 0, a, :, 3 * arr : 3 * arr + 3].reshape(tokens, 128) for a in range(4)], axis=1
        )

    gate_ref[...] = (jnp.dot(xt[...], gathered(1), preferred_element_type=F32) * factor).astype(BF)
    up_ref[...] = (jnp.dot(xt[...], gathered(2), preferred_element_type=F32) * factor).astype(BF)
    down_ref[...] = (lax.dot_general(gathered(0), dy[...], TN, preferred_element_type=F32) * factor).astype(BF)


def local(layer_input, out_grad, gate_weight, up_weight, down_weight):
    depth, width = gate_weight.shape
    blocks = width // BLOCK
    units = GROUPS * blocks
    any_spec = pl.BlockSpec(memory_space=pl.ANY)
    tile = (16, 128)
    input_grad, gathered, tokens = pl.pallas_call(
        stream_kernel,
        out_shape=(
            jax.ShapeDtypeStruct((HALF, depth), BF),
            jax.ShapeDtypeStruct((units, 4, 4, 9) + tile, BF),
            jax.ShapeDtypeStruct((GROUPS, 2, 2, HALF, depth), BF),
        ),
        in_specs=[any_spec] * 5,
        out_specs=(pl.BlockSpec(memory_space=pltpu.VMEM), any_spec, any_spec),
        scratch_shapes=[
            pltpu.VMEM((depth, width), BF),
            pltpu.VMEM((depth, width), BF),
            pltpu.VMEM((width, depth), BF),
            pltpu.VMEM((8, 2, HALF, depth), BF),
            pltpu.VMEM((SLOTS, 4, 4, 9) + tile, BF),
            pltpu.VMEM((SLOTS, 2, 2, 9) + tile, BF),
            pltpu.VMEM((SLOTS, 2, 4, 9) + tile, BF),
            pltpu.VMEM((SLOTS, 9) + tile, BF),
            pltpu.VMEM((SLOTS, 2, 9) + tile, BF),
            pltpu.VMEM((units, 4, 4, 9) + tile, BF),
            pltpu.VMEM((ROWS, depth), F32),
            pltpu.VMEM((GROUPS, 2, HALF, depth), BF),
            pltpu.VMEM((8, HALF, depth), BF),
            pltpu.SemaphoreType.DMA((3, blocks)),
            pltpu.SemaphoreType.DMA((2,)),
            pltpu.SemaphoreType.DMA((7,)),
            pltpu.SemaphoreType.DMA((8,)),
            pltpu.SemaphoreType.DMA((SLOTS, 16)),
            pltpu.SemaphoreType.DMA((SLOTS, 16)),
            pltpu.SemaphoreType.DMA((GROUPS, 2)),
            pltpu.SemaphoreType.DMA((8,)),
            pltpu.SemaphoreType.DMA((units,)),
            pltpu.SemaphoreType.DMA((GROUPS,)),
        ],
        compiler_params=pltpu.CompilerParams(
            collective_id=0, has_side_effects=True, vmem_limit_bytes=60 * 2**20
        ),
        name="stream",
    )(layer_input, out_grad, gate_weight, up_weight, down_weight)
    factor = 1.0 / (GROUPS * ROWS) ** 0.5
    gate_grad, up_grad, down_grad = pl.pallas_call(
        lambda *refs: weight_kernel(factor, *refs),
        grid=(blocks,),
        out_shape=(
            jax.ShapeDtypeStruct((depth, width), BF),
            jax.ShapeDtypeStruct((depth, width), BF),
            jax.ShapeDtypeStruct((width, depth), BF),
        ),
        in_specs=[
            pl.BlockSpec((GROUPS, 1, 4, 4, 9) + tile, lambda j: (0, j, 0, 0, 0, 0, 0)),
            pl.BlockSpec((GROUPS, 2, 2, HALF, depth), lambda j: (0, 0, 0, 0, 0)),
        ],
        out_specs=(
            pl.BlockSpec((depth, BLOCK), lambda j: (0, j)),
            pl.BlockSpec((depth, BLOCK), lambda j: (0, j)),
            pl.BlockSpec((BLOCK, depth), lambda j: (j, 0)),
        ),
        scratch_shapes=[
            pltpu.VMEM((depth, GROUPS * ROWS), BF),
            pltpu.VMEM((GROUPS * ROWS, depth), BF),
        ],
        compiler_params=pltpu.CompilerParams(vmem_limit_bytes=40 * 2**20),
        name="weight_grads",
    )(gathered.reshape((GROUPS, blocks, 4, 4, 9) + tile), tokens)
    return (input_grad, gate_grad, up_grad, down_grad)


def solution(mesh):
    placed = (P("col", "row"), P("col", "row"), P("row", "col"), P("row", "col"), P("col", "row"))
    return jax.shard_map(
        local,
        mesh=mesh,
        in_specs=placed,
        out_specs=(P("col", "row"), P("row", "col"), P("row", "col"), P("col", "row")),
        check_vma=False,
    )
```

time: 430 us -> 218 us (0.51)
  waiting for transfers between devices: 271 us -> 0 us
  Pallas kernels: 0 us -> 215 us
  matrix products: 56.3 us -> 0 us
  local copies, waits for them, and re-layouts: 34.2 us -> 2.05 us
  blocking collectives: 29.8 us -> 0 us
  other arithmetic: 21.2 us -> 0 us
  between operations: 13.8 us -> 0.65 us
    pallas_call x0 -> x2, Pallas kernels: none -> 215 us  [the longest x1 201 us: local(): pl.pallas_call(stream_kernel, out_shape=(jax.ShapeDtypeStruct((HALF, dept...]
    all_gather x3 -> x0, waiting for transfers between devices: 136 us -> none  [the longest x1 56.2 us: local(): lax.all_gather(gate_delta, 'row', axis=0, tiled=True)]
    reduce_scatter x2 -> x0, waiting for transfers between devices: 134 us -> none  [the longest x1 110 us: local(): lax.psum_scatter(jnp.concatenate([gate_up, hidden_grad], axis=1).astype(j...]
    dot_general x7 -> x0, matrix products: 56.3 us -> none  [the longest x1 13.8 us: local(): gate_up = jnp.dot(left, both_weights, preferred_element_type=jnp.float32)]
    unnamed x3 -> x5, local copies, waits for them, and re-layouts: 34.2 us -> 2.05 us
    all_gather x2 -> x0, blocking collectives: 29.8 us -> none  [the longest x1 16.1 us: local(): lax.all_gather(layer_input, 'col', axis=0, tiled=True)]
    concatenate x1 -> x0, other arithmetic: 18.5 us -> none  [local(): jnp.concatenate([gate_up, hidden_grad], axis=1).astype(jnp.bfloat16)]
  transfers between devices with their start and end apart: 5 -> 0, of which waited for: 5 -> 0; matrix products, arithmetic and copies ran while one was open for 11% -> 0% of each run, Pallas kernels for 0% -> 0%
where the time goes in v1:
time: 218 us
  Pallas kernels  215 us (99%)
    pallas_call x1, Pallas kernels, local(): pl.pallas_call(stream_kernel, out_shape=(jax.ShapeDtypeStruct((HALF, dept...  201 us
    pallas_call x1, Pallas kernels, local(): pl.pallas_call(lambda *refs: weight_kernel(factor, *refs), grid=(blocks,)...  14.1 us

profile of v1, /device:TPU:1, one launch (start us, length us, event | category | flops | bytes accessed | tf_op | source)
XLA Modules:
  0.0 217.8 jit_solution(13717173256269803272)
XLA Ops:
  0.6 201.0 %stream.1 = (bf16[96,512]{1,0:T(8,128)(2,1)}, bf16[28,4,4,9,16,128]{5,4,3,2,1,0:T(8,128)(2,1)}, bf16[4,2,2,96,512]{4,3,2,1,0:T(8,128)(2,1)}) custom-call(bf16[96,512]{1,0:T(8,128)(2,1)} %x_hbm.1, bf16[96,512]{1,0:T(8,128)(2,1)} %dy_hbm.1, bf16[512,3584]{1,0:T(8,128)(2,1)} %wg_hbm.1, bf16[512,3584]{1,0:T(8,128)(2,1)} %wu_hbm.1, bf16[3584,512]{1,0:T(8,128)(2,1)} %wd_hbm.1), custom_call_target="tpu_custom_call" | custom-call | tf_op jit(solution)/shard_map/stream/pallas_call | solution.py:323
  201.6 0.0 copy-start
  201.6 1.4 copy-done
  203.0 0.0 copy-start.1
  203.0 14.1 %weight_grads.1 = (bf16[512,3584]{1,0:T(8,128)(2,1)}, bf16[512,3584]{1,0:T(8,128)(2,1)}, bf16[3584,512]{1,0:T(8,128)(2,1)}) custom-call(bf16[4,7,4,4,9,16,128]{6,5,4,3,2,1,0:T(8,128)(2,1)} %bitcast.1, bf16[4,2,2,96,512]{4,3,2,1,0:T(8,128)(2,1)S(1)} %copy-done), custom_call_target="tpu_custom_call" | custom-call | tf_op jit(solution)/shard_map/weight_grads/pallas_call | solution.py:363
  217.2 0.0 copy-done.1
  217.2 0.6 copy.10
Async XLA Ops:
  201.6 1.4 copy-start
  203.0 14.1 %copy-start.1 = (bf16[96,512]{1,0:T(8,128)(2,1)S(1)}, bf16[96,512]{1,0:T(8,128)(2,1)}, u32[]{:S(2)}) copy-start(bf16[96,512]{1,0:T(8,128)(2,1)} %get-tuple-element.20) | copy-start | bytes 294916

commit v2 on v1

v2 whole, which is shorter than its diff:
```python
import functools

import jax
import jax.numpy as jnp
from jax import lax
from jax.experimental import pallas as pl
from jax.experimental.pallas import tpu as pltpu
from jax.sharding import PartitionSpec as P

MESH = pl.DeviceIdType.MESH
BF = jnp.bfloat16
F32 = jnp.float32
NT = (((1,), (1,)), ((), ()))
TN = (((0,), (0,)), ((), ()))
GROUPS = 4
ROWS = 192
HALF = 96
SIDE = 4
BLOCK = 512
SLOTS = 14
STAGES = (0, 2, 4, 6, 8, 10, 12, 14, 16)


def stream_kernel(
    factor, x_hbm, dy_hbm, wg_hbm, wu_hbm, wd_hbm,
    out_ref, wg, wu, wd,
    xb, xt, part, r1, r2, r3, r4, full, acc, stage, landed,
    w_sem, x_sem, xs_sem, xr_sem, ssem, rsem, is_sem, ir_sem,
):
    blocks = wg.shape[1] // BLOCK
    units = GROUPS * blocks
    row = lax.axis_index("row")
    col = lax.axis_index("col")
    y, x = row // SIDE, lax.rem(row, SIDE)
    z, core = col // 2, lax.rem(col, 2)

    def add(a, n):
        return lax.rem(a + n, 4)

    def weight_copies(j):
        cols = pl.ds(pl.multiple_of(j * BLOCK, BLOCK), BLOCK)
        return (
            pltpu.make_async_copy(wg_hbm.at[:, cols], wg.at[:, cols], w_sem.at[0, j]),
            pltpu.make_async_copy(wu_hbm.at[:, cols], wu.at[:, cols], w_sem.at[1, j]),
            pltpu.make_async_copy(wd_hbm.at[cols, :], wd.at[cols, :], w_sem.at[2, j]),
        )

    own = (
        pltpu.make_async_copy(x_hbm, xb.at[col, 0], x_sem.at[0]),
        pltpu.make_async_copy(dy_hbm, xb.at[col, 1], x_sem.at[1]),
    )
    for c in weight_copies(0) + own + weight_copies(1):
        c.start()

    partners = [(z, 1 - core)] + [(add(z, 4 - d), k) for d in (1, 2, 3) for k in (0, 1)]
    around = [(y, add(x, 1)), (y, add(x, 3)), (add(y, 1), x), (add(y, 3), x)]
    barrier = pltpu.get_barrier_semaphore()
    for pz, pk in partners:
        pl.semaphore_signal(barrier, inc=1, device_id=(row, pz * 2 + pk), device_id_type=MESH)
    for py, px in around:
        pl.semaphore_signal(barrier, inc=1, device_id=(py * SIDE + px, col), device_id_type=MESH)
    pl.semaphore_wait(barrier, len(partners) + len(around))

    def shard_copies(n, source):
        pz, pk = partners[n]
        return [
            pltpu.make_async_remote_copy(
                src_ref=ref, dst_ref=xb.at[source, h], send_sem=xs_sem.at[n, h], recv_sem=xr_sem.at[source, h],
                device_id=(row, pz * 2 + pk), device_id_type=MESH,
            )
            for h, ref in enumerate((x_hbm, dy_hbm))
        ]

    for n in range(len(partners)):
        for c in shard_copies(n, col):
            c.start()
    for c in own:
        c.wait()
    for c in shard_copies(0, z * 2 + 1 - core):
        c.wait_recv()

    def term_copy(s, k):
        return pltpu.make_async_remote_copy(
            src_ref=stage.at[s, k], dst_ref=landed.at[col], send_sem=is_sem.at[s, k], recv_sem=ir_sem.at[col],
            device_id=(row, add(z, s) * 2 + k), device_id_type=MESH,
        )

    @pl.loop(0, units + STAGES[-1])
    def _(t):
        def send(u, slot, m):
            even = lax.rem(u, 2) == 0
            i1, i2 = jnp.where(even, x, y), jnp.where(even, y, x)

            def device(d1, d2):
                a, b = add(i1, d1), add(i2, d2)
                return (jnp.where(even, b, a) * SIDE + jnp.where(even, a, b), col)

            up1, down1, up2, down2 = device(1, 0), device(3, 0), device(0, 1), device(0, 3)
            n1, p1, f1 = add(i1, 1), add(i1, 3), add(i1, 2)
            n2, p2, f2 = add(i2, 1), add(i2, 3), add(i2, 2)
            src, dst, target = {
                0: (lambda: part.at[slot, f1, pl.ds(0, 2)], lambda: r1.at[slot, 0], up1),
                1: (lambda: part.at[slot, f1, pl.ds(2, 2)], lambda: r1.at[slot, 1], down1),
                2: (lambda: part.at[slot, n1, pl.ds(0, 2)], lambda: r2.at[slot, 0, pl.ds(0, 2)], up1),
                3: (lambda: part.at[slot, p1, pl.ds(2, 2)], lambda: r2.at[slot, 1, pl.ds(2, 2)], down1),
                4: (lambda: part.at[slot, i1, f2, pl.ds(0, 5)], lambda: r3.at[slot, pl.ds(0, 5)], up2),
                5: (lambda: part.at[slot, i1, f2, pl.ds(5, 4)], lambda: r3.at[slot, pl.ds(5, 4)], down2),
                6: (lambda: part.at[slot, i1, n2], lambda: r4.at[slot, 0], up2),
                7: (lambda: part.at[slot, i1, p2], lambda: r4.at[slot, 1], down2),
                8: (lambda: full.at[u, i1, i2], lambda: full.at[u, i1, i2], up2),
                9: (lambda: full.at[u, i1, i2], lambda: full.at[u, i1, i2], down2),
                10: (lambda: full.at[u, i1, p2, pl.ds(0, 5)], lambda: full.at[u, i1, p2, pl.ds(0, 5)], up2),
                11: (lambda: full.at[u, i1, n2, pl.ds(5, 4)], lambda: full.at[u, i1, n2, pl.ds(5, 4)], down2),
                12: (lambda: full.at[u, i1, pl.ds(0, 2)], lambda: full.at[u, i1, pl.ds(0, 2)], up1),
                13: (lambda: full.at[u, i1, pl.ds(2, 2)], lambda: full.at[u, i1, pl.ds(2, 2)], down1),
                14: (lambda: full.at[u, p1, pl.ds(0, 2)], lambda: full.at[u, p1, pl.ds(0, 2)], up1),
                15: (lambda: full.at[u, n1, pl.ds(2, 2)], lambda: full.at[u, n1, pl.ds(2, 2)], down1),
                16: (lambda: part.at[slot, n1, pl.ds(2, 2)], lambda: r2.at[slot, 0, pl.ds(2, 2)], up1),
                17: (lambda: part.at[slot, p1, pl.ds(0, 2)], lambda: r2.at[slot, 1, pl.ds(0, 2)], down1),
                18: (lambda: full.at[u, i1, pl.ds(2, 2)], lambda: full.at[u, i1, pl.ds(2, 2)], up1),
                19: (lambda: full.at[u, i1, pl.ds(0, 2)], lambda: full.at[u, i1, pl.ds(0, 2)], down1),
            }[m]
            return pltpu.make_async_remote_copy(
                src_ref=src(), dst_ref=dst(), send_sem=ssem.at[slot, m], recv_sem=rsem.at[slot, m],
                device_id=target, device_id_type=MESH,
            )

        def at_stage(k):
            u = t - STAGES[k]

            def run(body):
                @pl.when(jnp.logical_and(u >= 0, u < units))
                def _():
                    even = lax.rem(u, 2) == 0
                    i1, i2 = jnp.where(even, x, y), jnp.where(even, y, x)
                    body(u, lax.rem(u, SLOTS), i1, i2)
            return run

        @at_stage(7)
        def _(u, slot, i1, i2):
            send(u, slot, 12).wait()
            send(u, slot, 14).start()
            send(u, slot, 13).wait()
            send(u, slot, 15).start()

        @at_stage(6)
        def _(u, slot, i1, i2):
            send(u, slot, 10).wait()
            send(u, slot, 11).wait()
            for m in (12, 13, 18, 19):
                send(u, slot, m).start()

        @at_stage(5)
        def _(u, slot, i1, i2):
            send(u, slot, 8).wait()
            send(u, slot, 10).start()
            send(u, slot, 9).wait()
            send(u, slot, 11).start()

        @at_stage(4)
        def _(u, slot, i1, i2):
            send(u, slot, 6).wait()
            send(u, slot, 7).wait()
            total = (
                part[slot, i1, i2].astype(F32) + r4[slot, 0].astype(F32) + r4[slot, 1].astype(F32)
            )
            gate, up, hidden_grad = total[0:3], total[3:6], total[6:9]
            sigma = 1.0 / (1.0 + jnp.exp(-gate))
            swish = gate * sigma
            full[u, i1, i2, 0:3] = (swish * up).astype(BF)
            full[u, i1, i2, 3:6] = (hidden_grad * up * sigma * (1.0 + gate * (1.0 - sigma))).astype(BF)
            full[u, i1, i2, 6:9] = (hidden_grad * swish).astype(BF)
            send(u, slot, 8).start()
            send(u, slot, 9).start()

        @at_stage(3)
        def _(u, slot, i1, i2):
            send(u, slot, 4).wait()
            part[slot, i1, add(i2, 1), 0:5] = (part[slot, i1, add(i2, 1), 0:5].astype(F32) + r3[slot, 0:5].astype(F32)).astype(BF)
            send(u, slot, 6).start()
            send(u, slot, 5).wait()
            part[slot, i1, add(i2, 3), 5:9] = (part[slot, i1, add(i2, 3), 5:9].astype(F32) + r3[slot, 5:9].astype(F32)).astype(BF)
            send(u, slot, 7).start()

        @at_stage(2)
        def _(u, slot, i1, i2):
            for m in (16, 17, 2, 3):
                send(u, slot, m).wait()
            part[slot, i1] = (
                part[slot, i1].astype(F32) + r2[slot, 0].astype(F32) + r2[slot, 1].astype(F32)
            ).astype(BF)
            send(u, slot, 4).start()
            send(u, slot, 5).start()

        @at_stage(1)
        def _(u, slot, i1, i2):
            send(u, slot, 0).wait()
            part[slot, add(i1, 1), 0:2] = (part[slot, add(i1, 1), 0:2].astype(F32) + r1[slot, 0].astype(F32)).astype(BF)
            send(u, slot, 2).start()
            send(u, slot, 1).wait()
            part[slot, add(i1, 3), 2:4] = (part[slot, add(i1, 3), 2:4].astype(F32) + r1[slot, 1].astype(F32)).astype(BF)
            send(u, slot, 3).start()

        @at_stage(0)
        def _(u, slot, i1, i2):
            s, j = u // blocks, lax.rem(u, blocks)
            group = add(z, s)

            @pl.when(s == 0)
            def _():
                for c in weight_copies(j):
                    c.wait()

                @pl.when(j + 2 < blocks)
                def _():
                    for c in weight_copies(j + 2):
                        c.start()

            @pl.when(jnp.logical_and(s > 0, j == 0))
            def _():
                for k in (0, 1):
                    for c in shard_copies(1, group * 2 + k):
                        c.wait_recv()

            @pl.when(jnp.logical_and(s == GROUPS - 1, j == 1))
            def _():
                for n in range(GROUPS):
                    xt[n] = xb[pl.ds(add(z, n) * 2, 2), 0].reshape(ROWS, BLOCK).T

            cols = pl.ds(pl.multiple_of(j * BLOCK, BLOCK), BLOCK)
            for arr in range(3):
                left = xb[pl.ds(group * 2, 2), arr // 2].reshape(ROWS, BLOCK)
                if arr == 0:
                    term = jnp.dot(left, wg[:, cols], preferred_element_type=F32)
                elif arr == 1:
                    term = jnp.dot(left, wu[:, cols], preferred_element_type=F32)
                else:
                    term = lax.dot_general(left, wd[cols, :], NT, preferred_element_type=F32)
                term = term.astype(BF)
                for a in range(4):
                    part[slot, a, :, 3 * arr : 3 * arr + 3] = term[:, 128 * a : 128 * a + 128].reshape(4, 3, 16, 128)
            for m in (0, 1, 16, 17):
                send(u, slot, m).start()

        @at_stage(8)
        def _(u, slot, i1, i2):
            s, j = u // blocks, lax.rem(u, blocks)
            for m in (18, 19, 14, 15):
                send(u, slot, m).wait()

            @pl.when(j == 0)
            def _():
                acc[...] = jnp.zeros_like(acc)

            cols = pl.ds(pl.multiple_of(j * BLOCK, BLOCK), BLOCK)
            total = acc[...]
            for arr, weight in ((1, wg), (2, wu)):
                left = jnp.concatenate(
                    [full[u, a, :, 3 * arr : 3 * arr + 3].reshape(ROWS, 128) for a in range(4)], axis=1
                )
                total = total + lax.dot_general(left, weight[:, cols], NT, preferred_element_type=F32)
            acc[...] = total

            @pl.when(j == blocks - 1)
            def _():
                for k in (0, 1):
                    mine = jnp.logical_and(s == 0, core == k)

                    @pl.when(mine)
                    def _():
                        landed[col] = acc[HALF * k : HALF * (k + 1)].astype(BF)

                    @pl.when(jnp.logical_not(mine))
                    def _():
                        stage[s, k] = acc[HALF * k : HALF * (k + 1)].astype(BF)
                        term_copy(s, k).start()

            @pl.when(s == GROUPS - 1)
            def _():
                def gathered(arr, n):
                    return jnp.concatenate(
                        [full[n * blocks + j, a, :, 3 * arr : 3 * arr + 3].reshape(ROWS, 128) for a in range(4)],
                        axis=1,
                    )

                for arr, grad in ((1, wg), (2, wu)):
                    total = jnp.dot(xt[0], gathered(arr, 0), preferred_element_type=F32)
                    for n in range(1, GROUPS):
                        total = total + jnp.dot(xt[n], gathered(arr, n), preferred_element_type=F32)
                    grad[:, cols] = (total * factor).astype(BF)
                hidden = jnp.concatenate([gathered(0, n) for n in range(GROUPS)], axis=0)
                right = jnp.concatenate(
                    [xb[pl.ds(add(z, n) * 2, 2), 1].reshape(ROWS, BLOCK) for n in range(GROUPS)], axis=0
                )
                wd[cols, :] = (lax.dot_general(hidden, right, TN, preferred_element_type=F32) * factor).astype(BF)

    total = landed[col].astype(F32)
    for pz, pk in partners:
        source = pz * 2 + pk
        pltpu.make_async_remote_copy(
            src_ref=stage.at[0, 0], dst_ref=landed.at[source], send_sem=is_sem.at[0, 0], recv_sem=ir_sem.at[source],
            device_id=(row, source), device_id_type=MESH,
        ).wait_recv()
        total = total + landed[source].astype(F32)
    out_ref[...] = total.astype(BF)

    for n in range(len(partners)):
        for c in shard_copies(n, col):
            c.wait_send()
    for s in range(GROUPS):
        for k in (0, 1):
            @pl.when(jnp.logical_not(jnp.logical_and(s == 0, core == k)))
            def _():
                term_copy(s, k).wait_send()


def local(layer_input, out_grad, gate_weight, up_weight, down_weight):
    depth, width = gate_weight.shape
    blocks = width // BLOCK
    units = GROUPS * blocks
    any_spec = pl.BlockSpec(memory_space=pl.ANY)
    tile = (16, 128)
    return pl.pallas_call(
        functools.partial(stream_kernel, 1.0 / (GROUPS * ROWS) ** 0.5),
        out_shape=(
            pltpu.VMEM((HALF, depth), BF),
            pltpu.VMEM((depth, width), BF),
            pltpu.VMEM((depth, width), BF),
            pltpu.VMEM((width, depth), BF),
        ),
        in_specs=[any_spec] * 5,
        out_specs=(pl.BlockSpec(memory_space=pltpu.VMEM),) * 4,
        scratch_shapes=[
            pltpu.VMEM((8, 2, HALF, depth), BF),
            pltpu.VMEM((GROUPS, depth, ROWS), BF),
            pltpu.VMEM((SLOTS, 4, 4, 9) + tile, BF),
            pltpu.VMEM((SLOTS, 2, 2, 9) + tile, BF),
            pltpu.VMEM((SLOTS, 2, 4, 9) + tile, BF),
            pltpu.VMEM((SLOTS, 9) + tile, BF),
            pltpu.VMEM((SLOTS, 2, 9) + tile, BF),
            pltpu.VMEM((units, 4, 4, 9) + tile, BF),
            pltpu.VMEM((ROWS, depth), F32),
            pltpu.VMEM((GROUPS, 2, HALF, depth), BF),
            pltpu.VMEM((8, HALF, depth), BF),
            pltpu.SemaphoreType.DMA((3, blocks)),
            pltpu.SemaphoreType.DMA((2,)),
            pltpu.SemaphoreType.DMA((7, 2)),
            pltpu.SemaphoreType.DMA((8, 2)),
            pltpu.SemaphoreType.DMA((SLOTS, 20)),
            pltpu.SemaphoreType.DMA((SLOTS, 20)),
            pltpu.SemaphoreType.DMA((GROUPS, 2)),
            pltpu.SemaphoreType.DMA((8,)),
        ],
        compiler_params=pltpu.CompilerParams(
            collective_id=0, has_side_effects=True, vmem_limit_bytes=48 * 2**20
        ),
        name="stream",
    )(layer_input, out_grad, gate_weight, up_weight, down_weight)


def solution(mesh):
    placed = (P("col", "row"), P("col", "row"), P("row", "col"), P("row", "col"), P("col", "row"))
    return jax.shard_map(
        local,
        mesh=mesh,
        in_specs=placed,
        out_specs=(P("col", "row"), P("row", "col"), P("row", "col"), P("col", "row")),
        check_vma=False,
    )
```

time: 218 us -> 203 us (0.931)
  Pallas kernels: 215 us -> 197 us
  local copies, waits for them, and re-layouts: 2.05 us -> 6.15 us
    pallas_call x2 -> x1, Pallas kernels: 215 us -> 197 us  [local(): pl.pallas_call(functools.partial(stream_kernel, 1.0 / (GROUPS * ROWS) **...]
    unnamed x5 -> x4, local copies, waits for them, and re-layouts: 2.05 us -> 6.15 us
where the time goes in v2:
time: 203 us
  Pallas kernels  197 us (97%)
  local copies, waits for them, and re-layouts  6.15 us (3%)
    pallas_call x1, Pallas kernels, local(): pl.pallas_call(functools.partial(stream_kernel, 1.0 / (GROUPS * ROWS) **...  197 us
    unnamed x4, local copies, waits for them, and re-layouts  6.15 us

profile of v2, /device:TPU:1, one launch (start us, length us, event | category | flops | bytes accessed | tf_op | source)
XLA Modules:
  0.0 203.4 jit_solution(2042107664406867332)
XLA Ops:
  0.6 196.6 %stream.1 = (bf16[96,512]{1,0:T(8,128)(2,1)S(1)}, bf16[512,3584]{1,0:T(8,128)(2,1)S(1)}, bf16[512,3584]{1,0:T(8,128)(2,1)S(1)}, bf16[3584,512]{1,0:T(8,128)(2,1)S(1)}) custom-call(bf16[96,512]{1,0:T(8,128)(2,1)} %x_hbm.1, bf16[96,512]{1,0:T(8,128)(2,1)} %dy_hbm.1, bf16[512,3584]{1,0:T(8,128)(2,1)} %wg_hbm.1, bf16[512,3584]{1,0:T(8,128)(2,1)} %wu_hbm.1, ...), custom_call_target="tpu_custom_call" | custom-call | tf_op jit(solution)/shard_map/stream/pallas_call | solution.py:323
  197.2 0.6 copy.13
  197.8 1.8 copy.14
  199.7 1.8 copy.15
  201.5 1.8 copy.16

commit v3 on v2

--- a/solution.py
+++ b/solution.py
@@ -18,6 +18,7 @@
 SIDE = 4
 BLOCK = 512
 SLOTS = 14
+TAIL = 2
 STAGES = (0, 2, 4, 6, 8, 10, 12, 14, 16)
 
 
@@ -37,6 +38,14 @@
     def add(a, n):
         return lax.rem(a + n, 4)
 
+    def group_and_block(u):
+        v = u - 2 * blocks
+        s = jnp.where(v < 0, jnp.where(u < blocks, 0, 2), 1 + 2 * lax.rem(jnp.maximum(v, 0), 2))
+        return s, jnp.where(v < 0, lax.rem(u, blocks), jnp.maximum(v, 0) // 2)
+
+    def unit_of(n, j):
+        return (j, 2 * blocks + 2 * j, blocks + j, 2 * blocks + 1 + 2 * j)[n]
+
     def weight_copies(j):
         cols = pl.ds(pl.multiple_of(j * BLOCK, BLOCK), BLOCK)
         return (
@@ -84,6 +93,26 @@
             src_ref=stage.at[s, k], dst_ref=landed.at[col], send_sem=is_sem.at[s, k], recv_sem=ir_sem.at[col],
             device_id=(row, add(z, s) * 2 + k), device_id_type=MESH,
         )
+
+    def weight_grads(j):
+        cols = pl.ds(pl.multiple_of(j * BLOCK, BLOCK), BLOCK)
+
+        def gathered(arr, n):
+            return jnp.concatenate(
+                [full[unit_of(n, j), a, :, 3 * arr : 3 * arr + 3].reshape(ROWS, 128) for a in range(4)],
+                axis=1,
+            )
+
+        for arr, grad in ((1, wg), (2, wu)):
+            total = jnp.dot(xt[0], gathered(arr, 0), preferred_element_type=F32)
+            for n in range(1, GROUPS):
+                total = total + jnp.dot(xt[n], gathered(arr, n), preferred_element_type=F32)
+            grad[:, cols] = (total * factor).astype(BF)
+        hidden = jnp.concatenate([gathered(0, n) for n in range(GROUPS)], axis=0)
+        right = jnp.concatenate(
+            [xb[pl.ds(add(z, n) * 2, 2), 1].reshape(ROWS, BLOCK) for n in range(GROUPS)], axis=0
+        )
+        wd[cols, :] = (lax.dot_general(hidden, right, TN, preferred_element_type=F32) * factor).astype(BF)
 
     @pl.loop(0, units + STAGES[-1])
     def _(t):
@@ -203,7 +232,7 @@
 
         @at_stage(0)
         def _(u, slot, i1, i2):
-            s, j = u // blocks, lax.rem(u, blocks)
+            s, j = group_and_block(u)
             group = add(z, s)
 
             @pl.when(s == 0)
@@ -244,22 +273,24 @@
 
         @at_stage(8)
         def _(u, slot, i1, i2):
-            s, j = u // blocks, lax.rem(u, blocks)
+            s, j = group_and_block(u)
             for m in (18, 19, 14, 15):
                 send(u, slot, m).wait()
 
+            which = s // 3
+
             @pl.when(j == 0)
             def _():
-                acc[...] = jnp.zeros_like(acc)
+                acc[which] = jnp.zeros((ROWS, BLOCK), F32)
 
             cols = pl.ds(pl.multiple_of(j * BLOCK, BLOCK), BLOCK)
-            total = acc[...]
+            total = acc[which]
             for arr, weight in ((1, wg), (2, wu)):
                 left = jnp.concatenate(
                     [full[u, a, :, 3 * arr : 3 * arr + 3].reshape(ROWS, 128) for a in range(4)], axis=1
                 )
                 total = total + lax.dot_general(left, weight[:, cols], NT, preferred_element_type=F32)
-            acc[...] = total
+            acc[which] = total
 
             @pl.when(j == blocks - 1)
             def _():
@@ -268,31 +299,20 @@
 
                     @pl.when(mine)
                     def _():
-                        landed[col] = acc[HALF * k : HALF * (k + 1)].astype(BF)
+                        landed[col] = acc[which, HALF * k : HALF * (k + 1)].astype(BF)
 
                     @pl.when(jnp.logical_not(mine))
                     def _():
-                        stage[s, k] = acc[HALF * k : HALF * (k + 1)].astype(BF)
+                        stage[s, k] = acc[which, HALF * k : HALF * (k + 1)].astype(BF)
                         term_copy(s, k).start()
 
-            @pl.when(s == GROUPS - 1)
-            def _():
-                def gathered(arr, n):
-                    return jnp.concatenate(
-                        [full[n * blocks + j, a, :, 3 * arr : 3 * arr + 3].reshape(ROWS, 128) for a in range(4)],
-                        axis=1,
-                    )
-
-                for arr, grad in ((1, wg), (2, wu)):
-                    total = jnp.dot(xt[0], gathered(arr, 0), preferred_element_type=F32)
-                    for n in range(1, GROUPS):
-                        total = total + jnp.dot(xt[n], gathered(arr, n), preferred_element_type=F32)
-                    grad[:, cols] = (total * factor).astype(BF)
-                hidden = jnp.concatenate([gathered(0, n) for n in range(GROUPS)], axis=0)
-                right = jnp.concatenate(
-                    [xb[pl.ds(add(z, n) * 2, 2), 1].reshape(ROWS, BLOCK) for n in range(GROUPS)], axis=0
-                )
-                wd[cols, :] = (lax.dot_general(hidden, right, TN, preferred_element_type=F32) * factor).astype(BF)
+            @pl.when(jnp.logical_and(s == GROUPS - 1, j < blocks - TAIL))
+            def _():
+                weight_grads(j)
+
+    @pl.loop(blocks - TAIL, blocks)
+    def _(j):
+        weight_grads(j)
 
     total = landed[col].astype(F32)
     for pz, pk in partners:
@@ -339,7 +359,7 @@
             pltpu.VMEM((SLOTS, 9) + tile, BF),
             pltpu.VMEM((SLOTS, 2, 9) + tile, BF),
             pltpu.VMEM((units, 4, 4, 9) + tile, BF),
-            pltpu.VMEM((ROWS, depth), F32),
+            pltpu.VMEM((2, ROWS, depth), F32),
             pltpu.VMEM((GROUPS, 2, HALF, depth), BF),
             pltpu.VMEM((8, HALF, depth), BF),
             pltpu.SemaphoreType.DMA((3, blocks)),

time: 203 us -> 201 us (level)
  Pallas kernels: 197 us -> 194 us
    pallas_call x1, Pallas kernels: 197 us -> 194 us  [local(): pl.pallas_call(functools.partial(stream_kernel, 1.0 / (GROUPS * ROWS) **...]
where the time goes in v3:
time: 201 us
  Pallas kernels  194 us (97%)
  local copies, waits for them, and re-layouts  6.15 us (3%)
    pallas_call x1, Pallas kernels, local(): pl.pallas_call(functools.partial(stream_kernel, 1.0 / (GROUPS * ROWS) **...  194 us
    unnamed x4, local copies, waits for them, and re-layouts  6.15 us

profile of v3, /device:TPU:1, one launch (start us, length us, event | category | flops | bytes accessed | tf_op | source)
XLA Modules:
  0.0 200.7 jit_solution(17614168099488573889)
XLA Ops:
  0.6 193.9 %stream.1 = (bf16[96,512]{1,0:T(8,128)(2,1)S(1)}, bf16[512,3584]{1,0:T(8,128)(2,1)S(1)}, bf16[512,3584]{1,0:T(8,128)(2,1)S(1)}, bf16[3584,512]{1,0:T(8,128)(2,1)S(1)}) custom-call(bf16[96,512]{1,0:T(8,128)(2,1)} %x_hbm.1, bf16[96,512]{1,0:T(8,128)(2,1)} %dy_hbm.1, bf16[512,3584]{1,0:T(8,128)(2,1)} %wg_hbm.1, bf16[512,3584]{1,0:T(8,128)(2,1)} %wu_hbm.1, ...), custom_call_target="tpu_custom_call" | custom-call | tf_op jit(solution)/shard_map/stream/pallas_call | solution.py:343
  194.5 0.6 copy.13
  195.2 1.8 copy.14
  197.0 1.8 copy.15
  198.8 1.8 copy.16

commit v4 on v3

--- a/solution.py
+++ b/solution.py
@@ -104,9 +104,8 @@
             )
 
         for arr, grad in ((1, wg), (2, wu)):
-            total = jnp.dot(xt[0], gathered(arr, 0), preferred_element_type=F32)
-            for n in range(1, GROUPS):
-                total = total + jnp.dot(xt[n], gathered(arr, n), preferred_element_type=F32)
+            right = jnp.concatenate([gathered(arr, n) for n in range(GROUPS)], axis=0)
+            total = jnp.dot(xt[...], right, preferred_element_type=F32)
             grad[:, cols] = (total * factor).astype(BF)
         hidden = jnp.concatenate([gathered(0, n) for n in range(GROUPS)], axis=0)
         right = jnp.concatenate(
@@ -253,8 +252,9 @@
 
             @pl.when(jnp.logical_and(s == GROUPS - 1, j == 1))
             def _():
-                for n in range(GROUPS):
-                    xt[n] = xb[pl.ds(add(z, n) * 2, 2), 0].reshape(ROWS, BLOCK).T
+                xt[...] = jnp.concatenate(
+                    [xb[pl.ds(add(z, n) * 2, 2), 0].reshape(ROWS, BLOCK) for n in range(GROUPS)], axis=0
+                ).T
 
             cols = pl.ds(pl.multiple_of(j * BLOCK, BLOCK), BLOCK)
             for arr in range(3):
@@ -352,7 +352,7 @@
         out_specs=(pl.BlockSpec(memory_space=pltpu.VMEM),) * 4,
         scratch_shapes=[
             pltpu.VMEM((8, 2, HALF, depth), BF),
-            pltpu.VMEM((GROUPS, depth, ROWS), BF),
+            pltpu.VMEM((depth, GROUPS * ROWS), BF),
             pltpu.VMEM((SLOTS, 4, 4, 9) + tile, BF),
             pltpu.VMEM((SLOTS, 2, 2, 9) + tile, BF),
             pltpu.VMEM((SLOTS, 2, 4, 9) + tile, BF),

time: 201 us -> 201 us (level)
  no operation moved by 1% of the time
where the time goes in v4:
time: 201 us
  Pallas kernels  194 us (97%)
  local copies, waits for them, and re-layouts  6.15 us (3%)
    pallas_call x1, Pallas kernels, local(): pl.pallas_call(functools.partial(stream_kernel, 1.0 / (GROUPS * ROWS) **...  194 us
    unnamed x4, local copies, waits for them, and re-layouts  6.15 us

profile of v4, /device:TPU:1, one launch (start us, length us, event | category | flops | bytes accessed | tf_op | source)
XLA Modules:
  0.0 200.7 jit_solution(15265120410157234196)
XLA Ops:
  0.6 193.9 %stream.1 = (bf16[96,512]{1,0:T(8,128)(2,1)S(1)}, bf16[512,3584]{1,0:T(8,128)(2,1)S(1)}, bf16[512,3584]{1,0:T(8,128)(2,1)S(1)}, bf16[3584,512]{1,0:T(8,128)(2,1)S(1)}) custom-call(bf16[96,512]{1,0:T(8,128)(2,1)} %x_hbm.1, bf16[96,512]{1,0:T(8,128)(2,1)} %dy_hbm.1, bf16[512,3584]{1,0:T(8,128)(2,1)} %wg_hbm.1, bf16[512,3584]{1,0:T(8,128)(2,1)} %wu_hbm.1, ...), custom_call_target="tpu_custom_call" | custom-call | tf_op jit(solution)/shard_map/stream/pallas_call | solution.py:343
  194.5 0.6 copy.13
  195.2 1.8 copy.14
  197.0 1.8 copy.15
  198.8 1.8 copy.16
